TPU v7x, 768 devices: a whole 4x8x12 slice. The times are simulated.
768 devices in a mesh: ctx: 32 (over y, z_hi), ulysses: 24 (over x, z_lo, core).
Axes of the slice: x: 4, y: 8, z: 12 (z_hi: 4, z_lo: 3; z = z_hi * 3 + z_lo), core: 2. Of those that a mesh axis runs over, the one named last changes fastest.
Arguments:
- queries: bfloat16 [98304, 6144], P(('ctx', 'ulysses')), may hold values from -120 to 120
- keys: bfloat16 [98304, 1024], P(('ctx', 'ulysses')), may hold values from -4 to 4
- values: bfloat16 [98304, 1024], P(('ctx', 'ulysses')), may hold values from -6 to 6
- doc_ids: int32 [98304], replicated, may hold values from 0 to 191, never falling along the last dimension, each value on 1 to 768 neighbouring positions
Outputs:
- attended: bfloat16 [98304, 6144], P(('ctx', 'ulysses'))
Inputs may be any that keep to these rules, and one draw needn't show every extreme that they name: `doc_ids`: document numbers never fall along the tokens; every document holds at most 768 tokens and one holds exactly that many.
All inputs are finite; a program needn't handle non-finite values.
Results may differ from a plain program's by a relative error of at most 0.001.
Values may be sent and summed in bfloat16 or wider, within the bound.
A program may use at most 64 MiB of HBM per device.

v0:
```python
import math

import jax
import jax.numpy as jnp
from jax import lax
from jax.sharding import PartitionSpec as P

HQ = 48
KV = 8
HEAD = 128


def from_behind(value, axis, steps):
    count = lax.axis_size(axis)
    leading, last = (max(0, -steps), min(count, count - steps))
    return lax.ppermute(value, axis, [(source, source + steps) for source in range(leading, last)])


def tile_length():
    return 512


def pack_heads(key_rows, value_rows, groups):
    local_tokens = key_rows.shape[0]
    copies = groups // KV
    key_send = jnp.repeat(key_rows.reshape(local_tokens, KV, HEAD), copies, axis=1)
    value_send = jnp.repeat(value_rows.reshape(local_tokens, KV, HEAD), copies, axis=1)
    return jnp.concatenate([key_send, value_send], axis=2).reshape(local_tokens, -1)


def shards(queries, keys, values, doc_ids):
    groups = lax.axis_size("ulysses")
    local_tokens = queries.shape[0]
    block_len = groups * local_tokens
    reach = block_len // 4
    query_slots = HQ // groups
    kv_slots = 1
    per_kv = query_slots // kv_slots
    kv_width = kv_slots * HEAD
    query_recv = lax.all_to_all(queries, "ulysses", split_axis=1, concat_axis=0, tiled=True)
    kv_block = lax.all_to_all(
        pack_heads(keys, values, groups), "ulysses", split_axis=1, concat_axis=0, tiled=True
    )
    query_rows = query_recv.reshape(block_len, kv_slots, per_kv, HEAD).transpose(1, 2, 0, 3)
    own_first = lax.axis_index("ctx") * block_len
    previous = from_behind(kv_block, "ctx", 1)
    tail_rows = previous[block_len - reach :]
    combined = jnp.concatenate([tail_rows, kv_block], axis=0)
    key_all = combined[:, :kv_width].reshape(-1, kv_slots, HEAD)
    value_all = combined[:, kv_width:].reshape(-1, kv_slots, HEAD)
    doc_pad = jnp.concatenate([jnp.full((reach,), -1, jnp.int32), doc_ids], axis=0)
    key_doc_all = lax.dynamic_slice_in_dim(doc_pad, own_first, reach + block_len, 0)
    query_doc = key_doc_all[reach:]
    query_len = tile_length()
    scale_factor = 1.0 / math.sqrt(HEAD)
    finished = []
    for query_start in range(0, block_len, query_len):
        tile_rows = query_rows[:, :, query_start : query_start + query_len]
        query_pos = own_first + query_start + jnp.arange(query_len, dtype=jnp.int32)
        tile_doc = query_doc[query_start : query_start + query_len]
        key_tile = key_all[query_start : query_start + reach + query_len]
        value_tile = value_all[query_start : query_start + reach + query_len]
        key_doc = key_doc_all[query_start : query_start + reach + query_len]
        key_pos = own_first - reach + query_start + jnp.arange(reach + query_len, dtype=jnp.int32)
        visible = (
            (key_doc[None, :] == tile_doc[:, None])
            & (key_pos[None, :] <= query_pos[:, None])
            & (key_pos[None, :] >= 0)
        )
        scores = (
            jnp.einsum("sgrd,ksd->sgrk", tile_rows, key_tile, preferred_element_type=jnp.float32)
            * scale_factor
        )
        masked = jnp.where(visible[None, None], scores, -1e30)
        peak = jnp.max(masked, axis=-1, keepdims=True)
        weights = jnp.where(visible[None, None], jnp.exp(scores - peak), 0.0)
        totals = jnp.sum(weights, axis=-1)
        mixed = jnp.einsum(
            "sgrk,ksd->sgrd",
            weights.astype(jnp.bfloat16),
            value_tile,
            preferred_element_type=jnp.float32,
        )
        finished.append((mixed / totals[..., None]).astype(jnp.bfloat16))
    output = jnp.concatenate(finished, axis=2)
    output = output.transpose(2, 0, 1, 3).reshape(block_len, query_slots * HEAD)
    return lax.all_to_all(output, "ulysses", split_axis=0, concat_axis=1, tiled=True)


def solution(mesh):
    placed = (
        P(("ctx", "ulysses"), None),
        P(("ctx", "ulysses"), None),
        P(("ctx", "ulysses"), None),
        P(),
    )
    return jax.shard_map(
        shards, mesh=mesh, in_specs=placed, out_specs=P(("ctx", "ulysses"), None), check_vma=False
    )
```

profile of v0, /device:TPU:57, one launch (start us, length us, event | category | flops | bytes accessed | tf_op | source)
XLA Modules:
  0.0 244.5 jit_solution(994708275896670503)
XLA Ops:
  0.0 0.0 copy-start
  0.0 0.9 copy-done
  1.0 1.0 copy_bitcast_fusion
  2.0 0.2 broadcast_in_dim.130
  2.2 0.2 broadcast_in_dim.131
  2.3 0.0 copy-start.1
  2.4 1.4 pad_maximum_fusion
  3.7 8.7 %all-to-all-start = ((bf16[128,24,256]{2,0,1:T(8,128)(2,1)}), bf16[128,24,256]{2,0,1:T(8,128)(2,1)S(1)}, u32[]{:S(2)}, u32[]{:S(2)}) async-start(bf16[128,24,256]{2,0,1:T(8,128)(2,1)} %pad_maximum_fusion), calls=%async_computation | async-start | bytes 3145728 | tf_op jit(solution)/shard_map/all_to_all | solution.py:41
  12.4 0.0 copy-done.1
  12.4 1.6 copy.39
  14.0 25.4 %all-to-all-done = bf16[128,24,256]{2,0,1:T(8,128)(2,1)S(1)} async-done(((bf16[128,24,256]{2,0,1:T(8,128)(2,1)}), bf16[128,24,256]{2,0,1:T(8,128)(2,1)S(1)}, u32[]{:S(2)}, u32[]{:S(2)}) %all-to-all-start) | async-done | bytes 1572896 | tf_op jit(solution)/shard_map/all_to_all | solution.py:41
  39.4 4.7 %all-to-all-start.1 = ((bf16[128,24,256]{0,2,1:T(8,128)(2,1)}), bf16[128,24,256]{0,2,1:T(8,128)(2,1)S(1)}, u32[]{:S(2)}, u32[]{:S(2)}) async-start(bf16[128,24,256]{0,2,1:T(8,128)(2,1)} %bitcast.5), calls=%async_computation.1 | async-start | bytes 3145728 | tf_op jit(solution)/shard_map/all_to_all | solution.py:40
  44.4 1.0 pad_dynamic-slice_fusion.11
  45.5 1.0 pad_dynamic-slice_fusion
  46.5 3.2 %and_and_fusion.4 = (pred[512,1280]{0,1:T(8,128)(4,1)}, pred[512,1280]{0,1:T(8,128)(4,1)}) fusion(s32[512]{0:T(512)S(1)} %iota_add_fusion.10, s32[512]{0:T(512)S(1)} %get-tuple-element.15, s32[1280]{0:T(1024)S(1)} %iota_add_fusion.4, s32[1280]{0:T(1024)S(1)} %get-tuple-element.9, pred[1280]{0:T(1024)(128)(4,1)S(1)} %broadcast_compare_fusion.4, ...), kind=kLoop, calls=%fused_computation.81 | loop fusion | flops 5242880 | bytes 1341952 | tf_op jit(solution)/shard_map/and | solution.py:66
  49.7 3.1 %and_and_fusion.2 = (pred[512,1280]{0,1:T(8,128)(4,1)}, pred[512,1280]{0,1:T(8,128)(4,1)}) fusion(s32[512]{0:T(512)S(1)} %iota_add_fusion.8, s32[512]{0:T(512)S(1)} %get-tuple-element.17, s32[1280]{0:T(1024)S(1)} %iota_add_fusion.2, s32[1280]{0:T(1024)S(1)} %get-tuple-element.11, pred[1280]{0:T(1024)(128)(4,1)S(1)} %broadcast_compare_fusion.2, ...), kind=kLoop, calls=%fused_computation.77 | loop fusion | flops 5242880 | bytes 1341952 | tf_op jit(solution)/shard_map/and | solution.py:66
  52.8 3.1 %and_and_fusion = (pred[512,1280]{0,1:T(8,128)(4,1)}, pred[512,1280]{0,1:T(8,128)(4,1)}) fusion(s32[512]{0:T(512)S(1)} %iota_add_fusion.6, s32[512]{0:T(512)S(1)} %get-tuple-element.13, s32[1280]{0:T(1024)S(1)} %iota_add_fusion, s32[1280]{0:T(1024)S(1)} %get-tuple-element.7, pred[1280]{0:T(1024)(128)(4,1)S(1)} %broadcast_compare_fusion, ...), kind=kLoop, calls=%fused_computation.73 | loop fusion | flops 5242880 | bytes 1341952 | tf_op jit(solution)/shard_map/and | solution.py:66
  55.9 10.0 %collective-permute-start = (bf16[3072,256]{1,0:T(8,128)(2,1)S(1)}, bf16[3072,256]{1,0:T(8,128)(2,1)}, u32[]{:S(2)}, u32[]{:S(2)}) collective-permute-start(bf16[3072,256]{1,0:T(8,128)(2,1)S(1)} %bitcast.282), channel_id=1, source_target_pairs={{0,24},{24,48},{48,72},{72,96},{96,120},{120,144},{144,168},{168,1... | collective-permute-start | bytes 4718600 | tf_op jit(solution)/shard_map/ppermute | solution.py:16
  65.9 5.2 %all-to-all-done.1 = bf16[128,24,256]{0,2,1:T(8,128)(2,1)S(1)} async-done(((bf16[128,24,256]{0,2,1:T(8,128)(2,1)}), bf16[128,24,256]{0,2,1:T(8,128)(2,1)S(1)}, u32[]{:S(2)}, u32[]{:S(2)}) %all-to-all-start.1) | async-done | bytes 1572896 | tf_op jit(solution)/shard_map/all_to_all | solution.py:40
  71.1 2.2 copy.40
  73.3 2.5 %reshape.725 = bf16[3072,1,2,128]{0,3,2,1:T(8,128)(2,1)S(1)} reshape(bf16[24,128,256]{1,0,2:T(8,128)(2,1)} %copy.40) | data formatting | bytes 3145728 | tf_op jit(solution)/shard_map/reshape | solution.py:44
  75.9 1.6 copy.41
  77.4 0.0 copy-start.2
  77.4 5.6 %fusion.171 = (f32[2,512]{1,0:T(2,128)S(1)}, bf16[2,512,1280]{1,2,0:T(8,128)(2,1)}) fusion(pred[512,1280]{0,1:T(8,128)(4,1)} %get-tuple-element.34, bf16[3072,256]{1,0:T(8,128)(2,1)S(1)} %bitcast.283, bf16[1,2,3072,128]{3,2,1,0:T(8,128)(2,1)} %bitcast.300), kind=kOutput, calls=%fused_computation.185 | convolution fusion | flops 680264960 | bytes 5115904 | tf_op jit(solution)/shard_map/sub | solution.py:76
  83.0 0.0 copy-done.2
  83.0 5.3 %fusion.172 = (f32[2,512]{1,0:T(2,128)S(1)}, bf16[2,512,1280]{1,2,0:T(8,128)(2,1)}) fusion(pred[512,1280]{0,1:T(8,128)(4,1)} %get-tuple-element.33, bf16[3072,256]{1,0:T(8,128)(2,1)S(1)} %bitcast.284, bf16[1,2,3072,128]{3,2,1,0:T(8,128)(2,1)S(1)} %bitcast.301), kind=kOutput, calls=%fused_computation.186 | convolution fusion | flops 680264960 | bytes 5115904 | tf_op jit(solution)/shard_map/sub | solution.py:76
  88.3 5.4 %fusion.173 = (f32[2,512]{1,0:T(2,128)S(1)}, bf16[2,512,1280]{1,2,0:T(8,128)(2,1)}) fusion(pred[512,1280]{0,1:T(8,128)(4,1)} %get-tuple-element.32, bf16[3072,256]{1,0:T(8,128)(2,1)S(1)} %bitcast.285, bf16[1,2,3072,128]{3,2,1,0:T(8,128)(2,1)S(1)} %bitcast.302), kind=kOutput, calls=%fused_computation.187 | convolution fusion | flops 680264960 | bytes 5115904 | tf_op jit(solution)/shard_map/sub | solution.py:76
  93.7 5.4 %fusion.174 = (f32[2,512]{1,0:T(2,128)S(1)}, bf16[2,512,1280]{1,2,0:T(8,128)(2,1)}) fusion(pred[512,1280]{0,1:T(8,128)(4,1)} %get-tuple-element.31, bf16[3072,256]{1,0:T(8,128)(2,1)S(1)} %bitcast.286, bf16[1,2,3072,128]{3,2,1,0:T(8,128)(2,1)S(1)} %bitcast.303), kind=kOutput, calls=%fused_computation.188 | convolution fusion | flops 680264960 | bytes 5115904 | tf_op jit(solution)/shard_map/sub | solution.py:76
  99.0 81.3 %collective-permute-done = bf16[3072,256]{1,0:T(8,128)(2,1)} collective-permute-done((bf16[3072,256]{1,0:T(8,128)(2,1)S(1)}, bf16[3072,256]{1,0:T(8,128)(2,1)}, u32[]{:S(2)}, u32[]{:S(2)}) %collective-permute-start) | collective-permute-done | bytes 1572896 | tf_op jit(solution)/shard_map/ppermute | solution.py:16
  180.3 1.0 slice.165
  181.3 0.0 copy-start.3
  181.4 0.7 copy-done.3
  182.1 0.9 maximum_bitcast_fusion
  183.0 5.8 %fusion.169 = (f32[2,512]{1,0:T(2,128)S(1)}, bf16[2,512,1280]{1,2,0:T(8,128)(2,1)}) fusion(bf16[1280,128,1]{1,0,2:T(8,128)(2,1)} %get-tuple-element.6, pred[512,1280]{0,1:T(8,128)(4,1)} %get-tuple-element.36, bf16[1,2,3072,128]{3,2,1,0:T(8,128)(2,1)S(1)} %bitcast.304), kind=kOutput, calls=%fused_computation.183 | convolution fusion | flops 680264960 | bytes 5115904 | tf_op jit(solution)/shard_map/sub | solution.py:76
  188.8 3.4 %fusion.111 = bf16[1,2,3072,128]{3,2,1,0:T(8,128)(2,1)} fusion(bf16[2,512,1280]{1,2,0:T(8,128)(2,1)} %get-tuple-element.20, bf16[3072,256]{1,0:T(8,128)(2,1)S(1)} %bitcast.288, bf16[768,256]{1,0:T(8,128)(2,1)} %copy-done.3, f32[2,512]{1,0:T(2,128)S(1)} %get-tuple-element.19), kind=kOutput, calls=%fused_computation.98 | convolution fusion | flops 336461824 | bytes 4853760 | tf_op jit(solution)/shard_map/sgrk,ksd->sgrd/dot_general | solution.py:78
  192.2 5.6 %fusion.170 = (f32[2,512]{1,0:T(2,128)S(1)}, bf16[2,512,1280]{1,2,0:T(8,128)(2,1)}) fusion(bf16[1280,128,1]{1,0,2:T(8,128)(2,1)} %get-tuple-element.5, pred[512,1280]{0,1:T(8,128)(4,1)} %get-tuple-element.35, bf16[1,2,3072,128]{3,2,1,0:T(8,128)(2,1)S(1)} %bitcast.305), kind=kOutput, calls=%fused_computation.184 | convolution fusion | flops 680264960 | bytes 5115904 | tf_op jit(solution)/shard_map/sub | solution.py:76
  197.7 0.0 copy-start.6
  197.7 3.5 %fusion.117 = bf16[1,2,3072,128]{3,2,1,0:T(8,128)(2,1)} fusion(bf16[1,2,3072,128]{3,2,1,0:T(8,128)(2,1)} %fusion.111, bf16[2,512,1280]{1,2,0:T(8,128)(2,1)} %get-tuple-element.22, bf16[3072,256]{1,0:T(8,128)(2,1)S(1)} %bitcast.289, bf16[768,256]{1,0:T(8,128)(2,1)} %copy-done.3, f32[2,512]{1,0:T(2,128)S(1)} %get-tuple-element.21), kind=kOutput, calls=%fused_computation.100 | convolution fusion | flops 336461824 | bytes 4853760 | tf_op jit(solution)/shard_map/sgrk,ksd->sgrd/dot_general | solution.py:78
  201.2 0.0 copy-done.6
  201.2 0.0 copy-start.7
  201.2 1.6 fusion.123
  202.9 0.1 copy-done.7
  203.0 0.0 copy-start.5
  203.0 1.6 fusion.129
  204.6 0.1 copy-done.5
  204.7 0.0 copy-start.4
  204.7 1.6 fusion.135
  206.3 0.1 copy-done.4
  206.5 1.6 fusion.141
  208.1 1.7 copy.48
  209.8 0.3 copy.59
  210.1 0.3 copy.49
  210.5 32.4 %all_to_all.51 = bf16[24,128,256]{1,2,0:T(8,128)(2,1)S(1)} all-to-all(bf16[24,128,256]{1,2,0:T(8,128)(2,1)S(1)} %copy.49), channel_id=1, replica_groups=mesh['ctx'=32,'ulysses'=24] {'ulysses'}, dimensions={0} | all-to-all | bytes 3145728 | tf_op jit(solution)/shard_map/all_to_all | solution.py:87
  242.9 1.6 copy.50
  (19 shorter events, 0.2 us)
Async XLA Ops:
  0.0 1.0 copy-start
  2.3 10.0 %copy-start.1 = (bf16[128,6144]{1,0:T(8,128)(2,1)S(1)}, bf16[128,6144]{1,0:T(8,128)(2,1)}, u32[]{:S(2)}) copy-start(bf16[128,6144]{1,0:T(8,128)(2,1)} %param.4) | copy-start | bytes 4718596
  3.7 35.7 %all-to-all-start = ((bf16[128,24,256]{2,0,1:T(8,128)(2,1)}), bf16[128,24,256]{2,0,1:T(8,128)(2,1)S(1)}, u32[]{:S(2)}, u32[]{:S(2)}) async-start(bf16[128,24,256]{2,0,1:T(8,128)(2,1)} %pad_maximum_fusion), calls=%async_computation | async-start | bytes 3145728 | tf_op jit(solution)/shard_map/all_to_all | solution.py:41
  39.4 31.8 %all-to-all-start.1 = ((bf16[128,24,256]{0,2,1:T(8,128)(2,1)}), bf16[128,24,256]{0,2,1:T(8,128)(2,1)S(1)}, u32[]{:S(2)}, u32[]{:S(2)}) async-start(bf16[128,24,256]{0,2,1:T(8,128)(2,1)} %bitcast.5), calls=%async_computation.1 | async-start | bytes 3145728 | tf_op jit(solution)/shard_map/all_to_all | solution.py:40
  55.9 124.4 %collective-permute-start = (bf16[3072,256]{1,0:T(8,128)(2,1)S(1)}, bf16[3072,256]{1,0:T(8,128)(2,1)}, u32[]{:S(2)}, u32[]{:S(2)}) collective-permute-start(bf16[3072,256]{1,0:T(8,128)(2,1)S(1)} %bitcast.282), channel_id=1, source_target_pairs={{0,24},{24,48},{48,72},{72,96},{96,120},{120,144},{144,168},{168,1... | collective-permute-start | bytes 4718600 | tf_op jit(solution)/shard_map/ppermute | solution.py:16
  77.4 5.6 %copy-start.2 = (bf16[3072,1,2,128]{3,0,2,1:T(8,128)(2,1)S(1)}, bf16[3072,1,2,128]{3,0,2,1:T(8,128)(2,1)}, u32[]{:S(2)}) copy-start(bf16[3072,1,2,128]{3,0,2,1:T(8,128)(2,1)} %copy.41) | copy-start | bytes 4718596
  181.3 0.7 copy-start.3
  197.7 3.5 %copy-start.6 = (bf16[2,512,1280]{1,2,0:T(8,128)(2,1)S(1)}, bf16[2,512,1280]{1,2,0:T(8,128)(2,1)}, u32[]{:S(2)}) copy-start(bf16[2,512,1280]{1,2,0:T(8,128)(2,1)} %get-tuple-element.24) | copy-start | bytes 7864324
  201.2 1.7 copy-start.7
  203.0 1.7 copy-start.5
  204.7 1.7 copy-start.4
where the time goes:
time: 245 us; the launch traced here: 244 us
  waiting for transfers between devices  112 us (46%)
  matrix products  46.4 us (19%)
  blocking collectives  32.4 us (13%)
  starting transfers between devices  23.4 us (10%)
  local copies, waits for them, and re-layouts  18.3 us (7%)
  other arithmetic  11.8 us (5%)
    ppermute x1, waiting for transfers between devices, from_behind(): lax.ppermute(value, axis, [(source, source + steps) for source in range(l...  81.3 us
    sub x6, matrix products, shards(): weights = jnp.where(visible[None, None], jnp.exp(scores - peak), 0.0)  33 us
    all_to_all x1, blocking collectives, shards(): lax.all_to_all(output, 'ulysses', split_axis=0, concat_axis=1, tiled=True)  32.4 us
    all_to_all x1, waiting for transfers between devices, shards(): lax.all_to_all(pack_heads(keys, values, groups), 'ulysses', split_axis=1,...  25.4 us
    dot_general x6, matrix products, shards(): jnp.einsum('sgrk,ksd->sgrd', weights.astype(jnp.bfloat16), value_tile, pr...  13.3 us
    ppermute x1, starting transfers between devices, from_behind(): lax.ppermute(value, axis, [(source, source + steps) for source in range(l...  10 us
    and x3, other arithmetic, shards(): (key_doc[None, :] == tile_doc[:, None]) & (key_pos[None, :] <= query_pos[...  9.39 us
    all_to_all x1, starting transfers between devices, shards(): lax.all_to_all(pack_heads(keys, values, groups), 'ulysses', split_axis=1,...  8.66 us
  transfers between devices with their start and end apart: 3, of which 3 were waited for; matrix products, arithmetic and copies ran while one was open for 17% of the time, Pallas kernels for 0%

commit v1 on v0

v1 whole, which is shorter than its diff:
```python
import math

import jax
import jax.numpy as jnp
from jax import lax
from jax.experimental import pallas as pl
from jax.experimental.pallas import tpu as pltpu
from jax.sharding import PartitionSpec as P

HQ = 48
KV = 8
HEAD = 128
PER = HQ // KV
CHUNK = 128
BACK = 6
SLOTS = BACK + 1
WINDOW = SLOTS * CHUNK
SCALE2 = math.log2(math.e) / math.sqrt(HEAD)
MESH = pl.DeviceIdType.MESH


def kernel(
    n_ctx, n_chip, q_hbm, k_hbm, v_hbm, doc_hbm, o_hbm,
    kv, qbuf, obuf, docs, bias, s_ref, p_ref,
    load_sem, q_sem, doc_sem, ici_send, pair_send, recv_sem, out_sem,
):
    ctx = lax.axis_index("ctx")
    uly = lax.axis_index("ulysses")
    lane = lax.rem(uly, 2)
    chip = ctx * n_chip + uly // 2
    chips = n_ctx * n_chip
    chunk = chip * 2 + lane
    ahead = lax.rem(chip + 1, chips)
    behind = lax.rem(chip + chips - 1, chips)
    next_id = (ahead // n_chip, lax.rem(ahead, n_chip) * 2 + lane)
    prev_id = (behind // n_chip, lax.rem(behind, n_chip) * 2 + lane)
    pair_id = (ctx, uly + 1 - 2 * lane)

    def own_load(h, part):
        src = (k_hbm, v_hbm)[part]
        return pltpu.make_async_copy(
            src.at[:, pl.ds(h * HEAD, HEAD)],
            kv.at[h, part, pl.ds(BACK * CHUNK, CHUNK), :],
            load_sem.at[part, h],
        )

    for h in range(KV):
        own_load(h, 0).start()
        own_load(h, 1).start()
    doc_load = pltpu.make_async_copy(doc_hbm, docs, doc_sem)
    doc_load.start()
    q_load = pltpu.make_async_copy(q_hbm, qbuf, q_sem)
    q_load.start()

    barrier = pltpu.get_barrier_semaphore()
    for who in (prev_id, pair_id):
        pl.semaphore_signal(barrier, inc=1, device_id=who, device_id_type=MESH)
    pl.semaphore_wait(barrier, 2)

    def rows(slot):
        return pl.ds(pl.multiple_of(slot * CHUNK, CHUNK), CHUNK)

    def hop(h, stage):
        src, dst = BACK - 2 * stage, BACK - 2 * stage - 2
        return pltpu.make_async_remote_copy(
            src_ref=kv.at[h, :, rows(src), :],
            dst_ref=kv.at[h, :, rows(dst), :],
            send_sem=ici_send.at[stage, h],
            recv_sem=recv_sem.at[dst, h],
            device_id=next_id,
            device_id_type=MESH,
        )

    def across(h, stage):
        src, dst = BACK - 2 * stage - 2 * lane, BACK - 2 * stage - 1
        return pltpu.make_async_remote_copy(
            src_ref=kv.at[h, :, rows(src), :],
            dst_ref=kv.at[h, :, rows(dst), :],
            send_sem=pair_send.at[stage, h],
            recv_sem=recv_sem.at[dst, h],
            device_id=pair_id,
            device_id_type=MESH,
        )

    def send_own(h):
        own_load(h, 0).wait()
        own_load(h, 1).wait()
        hop(h, 0).start()

    for h in range(2):
        send_own(h)

    doc_load.wait()
    own_doc = docs[pl.ds(chunk, 1), :]
    query_doc = jnp.transpose(jnp.broadcast_to(own_doc, (CHUNK, CHUNK)))
    row = lax.broadcasted_iota(jnp.int32, (CHUNK, CHUNK), 0)
    col = lax.broadcasted_iota(jnp.int32, (CHUNK, CHUNK), 1)
    for slot in range(SLOTS):
        where = chunk - (BACK - slot)
        key_doc = docs[pl.ds(jnp.maximum(where, 0), 1), :]
        visible = query_doc == jnp.broadcast_to(key_doc, (CHUNK, CHUNK))
        if slot == BACK:
            visible = visible & (col <= row)
        else:
            visible = visible & (jnp.broadcast_to(where, (CHUNK, CHUNK)) >= 0)
        bias[:, slot * CHUNK : (slot + 1) * CHUNK] = jnp.where(visible, 0.0, -1e30).astype(jnp.float32)
    q_load.wait()

    def out_copy(h):
        cols = pl.ds(pl.multiple_of(h * (PER * HEAD), PER * HEAD), PER * HEAD)
        return pltpu.make_async_copy(obuf.at[:, cols], o_hbm.at[:, cols], out_sem.at[h])

    def attend(h):
        base = h * (PER * HEAD)
        q_all = jnp.concatenate(
            [qbuf[:, pl.ds(pl.multiple_of(base + r * HEAD, HEAD), HEAD)] for r in range(PER)], axis=0
        )
        for first in range(0, WINDOW, 256):
            width = min(256, WINDOW - first)
            block = lax.dot_general(
                q_all, kv[h, 0, first : first + width, :], (((1,), (1,)), ((), ())),
                preferred_element_type=jnp.float32,
            )
            for r in range(PER):
                s_ref[r * CHUNK : (r + 1) * CHUNK, first : first + width] = (
                    block[r * CHUNK : (r + 1) * CHUNK] + bias[:, first : first + width]
                )
        totals = []
        step = 32
        for r in range(0, PER * CHUNK, step):
            scores = s_ref[r : r + step, :]
            peak = jnp.max(scores, axis=-1, keepdims=True)
            weights = jnp.exp2((scores - peak) * SCALE2)
            totals.append(jnp.sum(weights, axis=-1, keepdims=True))
            p_ref[r : r + step, :] = weights.astype(jnp.bfloat16)
        mixed = jnp.dot(p_ref[...], kv[h, 1], preferred_element_type=jnp.float32)
        done = (mixed / jnp.concatenate(totals, axis=0)).astype(jnp.bfloat16)
        for r in range(PER):
            obuf[:, pl.ds(pl.multiple_of(base + r * HEAD, HEAD), HEAD)] = done[r * CHUNK : (r + 1) * CHUNK]
        out_copy(h).start()

    def step(t, carry):
        @pl.when(t + 2 < KV)
        def _():
            send_own(t + 2)

        @pl.when(t < KV)
        def _():
            hop(t, 0).wait_recv()
            hop(t, 1).start()
            across(t, 0).start()

        @pl.when((t >= 1) & (t < KV + 1))
        def _():
            h = t - 1
            hop(h, 1).wait_recv()
            hop(h, 2).start()
            across(h, 1).start()

        @pl.when((t >= 2) & (t < KV + 2))
        def _():
            h = t - 2
            hop(h, 2).wait_recv()
            across(h, 2).start()

        @pl.when(t >= 3)
        def _():
            h = t - 3
            for stage in range(3):
                across(h, stage).wait_recv()
            attend(h)

        return carry

    lax.fori_loop(0, KV + 3, step, 0)

    def drain(h, carry):
        for stage in range(3):
            hop(h, stage).wait_send()
            across(h, stage).wait_send()
        out_copy(h).wait()
        return carry

    lax.fori_loop(0, KV, drain, 0)


def shards(n_ctx, n_chip, queries, keys, values, doc_ids):
    tokens = queries.shape[0]
    anywhere = pl.BlockSpec(memory_space=pl.ANY)
    docs = doc_ids.reshape(-1, CHUNK)
    return pl.pallas_call(
        lambda *refs: kernel(n_ctx, n_chip, *refs),
        out_shape=jax.ShapeDtypeStruct((tokens, HQ * HEAD), jnp.bfloat16),
        in_specs=[anywhere] * 4,
        out_specs=anywhere,
        scratch_shapes=[
            pltpu.VMEM((KV, 2, WINDOW, HEAD), jnp.bfloat16),
            pltpu.VMEM((CHUNK, HQ * HEAD), jnp.bfloat16),
            pltpu.VMEM((CHUNK, HQ * HEAD), jnp.bfloat16),
            pltpu.VMEM(docs.shape, jnp.int32),
            pltpu.VMEM((CHUNK, WINDOW), jnp.float32),
            pltpu.VMEM((PER * CHUNK, WINDOW), jnp.float32),
            pltpu.VMEM((PER * CHUNK, WINDOW), jnp.bfloat16),
            pltpu.SemaphoreType.DMA((2, KV)),
            pltpu.SemaphoreType.DMA,
            pltpu.SemaphoreType.DMA,
            pltpu.SemaphoreType.DMA((3, KV)),
            pltpu.SemaphoreType.DMA((3, KV)),
            pltpu.SemaphoreType.DMA((BACK, KV)),
            pltpu.SemaphoreType.DMA((KV,)),
        ],
        compiler_params=pltpu.CompilerParams(
            collective_id=0, has_side_effects=True, vmem_limit_bytes=56 * 1024 * 1024
        ),
        name="halo_attention",
    )(queries, keys, values, docs)


def solution(mesh):
    placed = (
        P(("ctx", "ulysses"), None),
        P(("ctx", "ulysses"), None),
        P(("ctx", "ulysses"), None),
        P(),
    )
    n_ctx, n_chip = mesh.shape["ctx"], mesh.shape["ulysses"] // 2
    return jax.shard_map(
        lambda *arrays: shards(n_ctx, n_chip, *arrays),
        mesh=mesh, in_specs=placed, out_specs=P(("ctx", "ulysses"), None), check_vma=False,
    )
```

time: 245 us -> 65.9 us (0.27)
  the two profiles are of different devices: /device:TPU:57 before, /device:TPU:1 now
where the time goes in v1:
time: 65.9 us; the launch traced here: 65.8 us
  Pallas kernels  63.1 us (96%)
  local copies, waits for them, and re-layouts  2.69 us (4%)
    pallas_call x1, Pallas kernels, shards(): pl.pallas_call(lambda *refs: kernel(n_ctx, n_chip, *refs), out_shape=jax....  63.1 us
    unnamed x1, local copies, waits for them, and re-layouts  2.69 us

profile of v1, /device:TPU:1, one launch (start us, length us, event | category | flops | bytes accessed | tf_op | source)
XLA Modules:
  0.0 65.8 jit_solution(5578850925353666044)
XLA Ops:
  0.0 63.1 %halo_attention.1 = bf16[128,6144]{1,0:T(8,128)(2,1)} custom-call(bf16[128,6144]{1,0:T(8,128)(2,1)} %refs_0_.1, bf16[128,1024]{1,0:T(8,128)(2,1)} %refs_1_.1, bf16[128,1024]{1,0:T(8,128)(2,1)} %refs_2_.1, s32[768,128]{1,0:T(8,128)} %bitcast.1), custom_call_target="tpu_custom_call" | custom-call | tf_op jit(solution)/shard_map/halo_attention/pallas_call | solution.py:191
  63.1 2.7 %copy.6 = bf16[128,6144]{1,0:T(8,128)(2,1)} copy(bf16[128,6144]{1,0:T(8,128)(2,1)} %halo_attention.1) | data formatting | bytes 3145728

commit v2 on v1

--- a/solution.py
+++ b/solution.py
@@ -16,58 +16,99 @@
 SLOTS = BACK + 1
 WINDOW = SLOTS * CHUNK
 SCALE2 = math.log2(math.e) / math.sqrt(HEAD)
+RUN = 3
+LAGS_IN = (0, 2, 1, 3)
+LAGS_TOP = (1, 3, 5, 6)
+LAGS_HELD = (3, 1, 0)
 MESH = pl.DeviceIdType.MESH
 
 
 def kernel(
     n_ctx, n_chip, q_hbm, k_hbm, v_hbm, doc_hbm, o_hbm,
-    kv, qbuf, obuf, docs, bias, s_ref, p_ref,
-    load_sem, q_sem, doc_sem, ici_send, pair_send, recv_sem, out_sem,
+    kv, held, qbuf, obuf, docs, bias, s_ref, p_ref,
+    load_sem, q_sem, doc_sem, push_send, held_send, pair_send, recv_sem, held_recv, out_sem,
 ):
     ctx = lax.axis_index("ctx")
     uly = lax.axis_index("ulysses")
     lane = lax.rem(uly, 2)
-    chip = ctx * n_chip + uly // 2
-    chips = n_ctx * n_chip
+    place = uly // 2
+    row, col = place // RUN, lax.rem(place, RUN)
+    last_row = n_chip // RUN - 1
+    chip = ctx * n_chip + place
     chunk = chip * 2 + lane
-    ahead = lax.rem(chip + 1, chips)
-    behind = lax.rem(chip + chips - 1, chips)
-    next_id = (ahead // n_chip, lax.rem(ahead, n_chip) * 2 + lane)
-    prev_id = (behind // n_chip, lax.rem(behind, n_chip) * 2 + lane)
+    top, inner = row == 0, row > 0
+    edge = (row == last_row) & (col == RUN - 1)
+    onward = ctx < n_ctx - 1
+    edge_far = edge & onward & (lane == 0)
+    edge_near = edge & onward & (lane == 1)
+    keeper = top & (col == RUN - 1) & onward & (lane == 0)
+    holder = chip - (n_chip - RUN)
+    after = chip + (n_chip - RUN + 1)
+
+    def core(target):
+        return (target // n_chip, lax.rem(target, n_chip) * 2 + lane)
+
     pair_id = (ctx, uly + 1 - 2 * lane)
 
     def own_load(h, part):
         src = (k_hbm, v_hbm)[part]
         return pltpu.make_async_copy(
-            src.at[:, pl.ds(h * HEAD, HEAD)],
+            src.at[:, pl.ds(pl.multiple_of(h * HEAD, HEAD), HEAD)],
             kv.at[h, part, pl.ds(BACK * CHUNK, CHUNK), :],
             load_sem.at[part, h],
         )
 
-    for h in range(KV):
+    def start_loads(h, carry):
         own_load(h, 0).start()
         own_load(h, 1).start()
+        return carry
+
+    lax.fori_loop(0, KV, start_loads, 0)
     doc_load = pltpu.make_async_copy(doc_hbm, docs, doc_sem)
     doc_load.start()
     q_load = pltpu.make_async_copy(q_hbm, qbuf, q_sem)
     q_load.start()
 
-    barrier = pltpu.get_barrier_semaphore()
-    for who in (prev_id, pair_id):
-        pl.semaphore_signal(barrier, inc=1, device_id=who, device_id_type=MESH)
-    pl.semaphore_wait(barrier, 2)
+    @pl.when(chip < 3)
+    def _():
+        def clear(h, carry):
+            for part in range(2):
+                kv[h, part, : BACK * CHUNK, :] = jnp.zeros((BACK * CHUNK, HEAD), jnp.bfloat16)
+            return carry
+
+        lax.fori_loop(0, KV, clear, 0)
 
     def rows(slot):
         return pl.ds(pl.multiple_of(slot * CHUNK, CHUNK), CHUNK)
 
-    def hop(h, stage):
-        src, dst = BACK - 2 * stage, BACK - 2 * stage - 2
+    def push(h, src, dst, index, target):
         return pltpu.make_async_remote_copy(
             src_ref=kv.at[h, :, rows(src), :],
             dst_ref=kv.at[h, :, rows(dst), :],
-            send_sem=ici_send.at[stage, h],
+            send_sem=push_send.at[index, h],
             recv_sem=recv_sem.at[dst, h],
-            device_id=next_id,
+            device_id=core(target),
+            device_id_type=MESH,
+        )
+
+    def push_held(h, src, index):
+        return pltpu.make_async_remote_copy(
+            src_ref=kv.at[h, :, rows(src), :],
+            dst_ref=held.at[h, src // 2 - 1],
+            send_sem=push_send.at[index, h],
+            recv_sem=held_recv.at[src // 2 - 1, h],
+            device_id=core(holder),
+            device_id_type=MESH,
+        )
+
+    def release(h, index):
+        dst = 2 * index
+        return pltpu.make_async_remote_copy(
+            src_ref=held.at[h, index],
+            dst_ref=kv.at[h, :, rows(dst), :],
+            send_sem=held_send.at[index, h],
+            recv_sem=recv_sem.at[dst, h],
+            device_id=core(after),
             device_id_type=MESH,
         )
 
@@ -82,25 +123,87 @@
             device_id_type=MESH,
         )
 
+    own_next = jnp.logical_not(edge) | edge_near
+    own_row = row < last_row
+    own_skip = (col == RUN - 1) & (own_row | edge_near)
+    relay_up = (col == 1) | (top & (col == 0) & (lane == 0)) | edge_near
+    relay_two = edge_near
+    relay_three = (top & (col == 1)) | (top & (col == 0) & (lane == 0)) | edge_near
+    relay_down = inner & (col == 1)
+
+    barrier = pltpu.get_barrier_semaphore()
+
+    def greet(cond, target):
+        @pl.when(cond)
+        def _():
+            pl.semaphore_signal(barrier, inc=1, device_id=core(target), device_id_type=MESH)
+
+    head_of_block = top & (col == 0)
+    has_back = ctx > 0
+    greet((chip >= 1) & jnp.logical_not(head_of_block & (lane == 0)), chip - 1)
+    greet(inner, chip - RUN)
+    greet((inner & (col == 1)) | (top & (col == 1) & has_back & (lane == 1)), chip - 2)
+    greet(inner & (col == 0), chip + 1)
+    greet(keeper, chip + (n_chip - RUN))
+    greet(head_of_block & has_back & (lane == 0), chip - (n_chip - RUN + 1))
+    pl.semaphore_signal(barrier, inc=1, device_id=pair_id, device_id_type=MESH)
+    expected = (
+        1
+        + own_next.astype(jnp.int32)
+        + own_row.astype(jnp.int32)
+        + own_skip.astype(jnp.int32)
+        + relay_down.astype(jnp.int32)
+        + edge_far.astype(jnp.int32)
+        + keeper.astype(jnp.int32)
+    )
+    pl.semaphore_wait(barrier, expected)
+
     def send_own(h):
         own_load(h, 0).wait()
         own_load(h, 1).wait()
-        hop(h, 0).start()
-
-    for h in range(2):
+
+        @pl.when(own_next)
+        def _():
+            push(h, 6, 4, 0, chip + 1).start()
+
+        @pl.when(edge_far)
+        def _():
+            push_held(h, 6, 0).start()
+
+        @pl.when(own_skip)
+        def _():
+            push(h, 6, 2, 2, chip + 2).start()
+
+        @pl.when(own_row)
+        def _():
+            push(h, 6, 0, 1, chip + 3).start()
+
+        @pl.when(lane == 0)
+        def _():
+            across(h, 0).start()
+
+    def received(h, slot):
+        push(h, 6, slot, 0, chip).wait_recv()
+
+    upfront = jnp.where((col == 1) & inner, 2, KV)
+
+    def first_sends(h, carry):
         send_own(h)
+        return carry
+
+    lax.fori_loop(0, upfront, first_sends, 0)
 
     doc_load.wait()
     own_doc = docs[pl.ds(chunk, 1), :]
     query_doc = jnp.transpose(jnp.broadcast_to(own_doc, (CHUNK, CHUNK)))
-    row = lax.broadcasted_iota(jnp.int32, (CHUNK, CHUNK), 0)
-    col = lax.broadcasted_iota(jnp.int32, (CHUNK, CHUNK), 1)
+    i = lax.broadcasted_iota(jnp.int32, (CHUNK, CHUNK), 0)
+    j = lax.broadcasted_iota(jnp.int32, (CHUNK, CHUNK), 1)
     for slot in range(SLOTS):
         where = chunk - (BACK - slot)
         key_doc = docs[pl.ds(jnp.maximum(where, 0), 1), :]
         visible = query_doc == jnp.broadcast_to(key_doc, (CHUNK, CHUNK))
         if slot == BACK:
-            visible = visible & (col <= row)
+            visible = visible & (j <= i)
         else:
             visible = visible & (jnp.broadcast_to(where, (CHUNK, CHUNK)) >= 0)
         bias[:, slot * CHUNK : (slot + 1) * CHUNK] = jnp.where(visible, 0.0, -1e30).astype(jnp.float32)
@@ -139,45 +242,115 @@
             obuf[:, pl.ds(pl.multiple_of(base + r * HEAD, HEAD), HEAD)] = done[r * CHUNK : (r + 1) * CHUNK]
         out_copy(h).start()
 
+    def on_near(h):
+        @pl.when(chip >= 1)
+        def _():
+            received(h, 4)
+
+            @pl.when(relay_up)
+            def _():
+                push(h, 4, 2, 3, chip + 1).start()
+
+            @pl.when(edge_far)
+            def _():
+                push_held(h, 4, 3).start()
+
+            @pl.when(relay_two)
+            def _():
+                push(h, 4, 0, 4, chip + 2).start()
+
+            across(h, 1 - lane).start()
+
+    def on_middle(h):
+        @pl.when(chip >= 2)
+        def _():
+            received(h, 2)
+
+            @pl.when(relay_three)
+            def _():
+                push(h, 2, 0, 5, chip + 1).start()
+
+            @pl.when(edge_far)
+            def _():
+                push_held(h, 2, 5).start()
+
+            across(h, 2 - lane).start()
+
+    def on_far(h):
+        @pl.when(chip >= 3)
+        def _():
+            received(h, 0)
+
+            @pl.when(relay_down)
+            def _():
+                push(h, 0, 2, 6, chip - 1).start()
+
+            @pl.when(lane == 1)
+            def _():
+                across(h, 2).start()
+
+    def on_held(h, index):
+        push_held(h, 2 * index + 2, 0).wait_recv()
+        release(h, index).start()
+
+    def inside(h):
+        return (h >= 0) & (h < KV)
+
+    def at(t, lag, action, extra=None):
+        h = t - lag
+        cond = inside(h) if extra is None else inside(h) & extra
+
+        @pl.when(cond)
+        def _():
+            action(h)
+
+    lag_near = jnp.where(top, LAGS_TOP[0], LAGS_IN[0])
+    lag_middle = jnp.where(top, LAGS_TOP[1], LAGS_IN[1])
+    lag_far = jnp.where(top, LAGS_TOP[2], LAGS_IN[2])
+    lag_attend = jnp.where(top, LAGS_TOP[3], LAGS_IN[3])
+
+    def finish(h):
+        for stage in range(3):
+            @pl.when(chip >= stage + 1 - lane)
+            def _():
+                across(h, stage).wait_recv()
+        attend(h)
+
     def step(t, carry):
-        @pl.when(t + 2 < KV)
-        def _():
-            send_own(t + 2)
-
-        @pl.when(t < KV)
-        def _():
-            hop(t, 0).wait_recv()
-            hop(t, 1).start()
-            across(t, 0).start()
-
-        @pl.when((t >= 1) & (t < KV + 1))
-        def _():
-            h = t - 1
-            hop(h, 1).wait_recv()
-            hop(h, 2).start()
-            across(h, 1).start()
-
-        @pl.when((t >= 2) & (t < KV + 2))
-        def _():
-            h = t - 2
-            hop(h, 2).wait_recv()
-            across(h, 2).start()
-
-        @pl.when(t >= 3)
-        def _():
-            h = t - 3
-            for stage in range(3):
-                across(h, stage).wait_recv()
-            attend(h)
-
+        at(t, -upfront, send_own)
+        at(t, lag_near, on_near)
+        at(t, LAGS_HELD[2], lambda h: on_held(h, 2), keeper)
+        at(t, LAGS_HELD[1], lambda h: on_held(h, 1), keeper)
+        at(t, LAGS_HELD[0], lambda h: on_held(h, 0), keeper)
+        at(t, lag_far, on_far, inner)
+        at(t, lag_middle, on_middle)
+        at(t, lag_far, on_far, top)
+        at(t, lag_attend, finish)
         return carry
 
-    lax.fori_loop(0, KV + 3, step, 0)
+    lax.fori_loop(0, KV + lag_attend, step, 0)
 
     def drain(h, carry):
+        sends = (
+            (0, own_next | edge_far), (1, own_row), (2, own_skip),
+            (3, (chip >= 1) & (relay_up | edge_far)), (4, relay_two),
+            (5, (chip >= 2) & (relay_three | edge_far)), (6, relay_down),
+        )
+        for index, cond in sends:
+            @pl.when(cond)
+            def _():
+                push(h, 6, 4, index, chip).wait_send()
+
+        for index in range(3):
+            @pl.when(keeper)
+            def _():
+                release(h, index).wait_send()
+
         for stage in range(3):
-            hop(h, stage).wait_send()
-            across(h, stage).wait_send()
+            @pl.when(chip >= stage + lane)
+            def _():
+                across(h, stage).wait_send()
+
         out_copy(h).wait()
         return carry
 
@@ -195,6 +368,7 @@
         out_specs=anywhere,
         scratch_shapes=[
             pltpu.VMEM((KV, 2, WINDOW, HEAD), jnp.bfloat16),
+            pltpu.VMEM((KV, 3, 2, CHUNK, HEAD), jnp.bfloat16),
             pltpu.VMEM((CHUNK, HQ * HEAD), jnp.bfloat16),
             pltpu.VMEM((CHUNK, HQ * HEAD), jnp.bfloat16),
             pltpu.VMEM(docs.shape, jnp.int32),
@@ -204,9 +378,11 @@
             pltpu.SemaphoreType.DMA((2, KV)),
             pltpu.SemaphoreType.DMA,
             pltpu.SemaphoreType.DMA,
+            pltpu.SemaphoreType.DMA((7, KV)),
             pltpu.SemaphoreType.DMA((3, KV)),
             pltpu.SemaphoreType.DMA((3, KV)),
             pltpu.SemaphoreType.DMA((BACK, KV)),
+            pltpu.SemaphoreType.DMA((3, KV)),
             pltpu.SemaphoreType.DMA((KV,)),
         ],
         compiler_params=pltpu.CompilerParams(

time: 65.9 us -> 60.7 us (0.921)
  the two profiles are of different devices: /device:TPU:1 before, /device:TPU:40 now
where the time goes in v2:
time: 60.7 us; the launch traced here: 60.5 us
  Pallas kernels  57.8 us (95%)
  local copies, waits for them, and re-layouts  2.69 us (4%)
    pallas_call x1, Pallas kernels, shards(): pl.pallas_call(lambda *refs: kernel(n_ctx, n_chip, *refs), out_shape=jax....  57.8 us
    unnamed x1, local copies, waits for them, and re-layouts  2.69 us

profile of v2, /device:TPU:40, one launch (start us, length us, event | category | flops | bytes accessed | tf_op | source)
XLA Modules:
  0.0 60.5 jit_solution(17306485753484220713)
XLA Ops:
  0.0 57.8 %halo_attention.1 = bf16[128,6144]{1,0:T(8,128)(2,1)} custom-call(bf16[128,6144]{1,0:T(8,128)(2,1)} %refs_0_.1, bf16[128,1024]{1,0:T(8,128)(2,1)} %refs_1_.1, bf16[128,1024]{1,0:T(8,128)(2,1)} %refs_2_.1, s32[768,128]{1,0:T(8,128)} %bitcast.1), custom_call_target="tpu_custom_call" | custom-call | tf_op jit(solution)/shard_map/halo_attention/pallas_call | solution.py:364
  57.8 2.7 %copy.6 = bf16[128,6144]{1,0:T(8,128)(2,1)} copy(bf16[128,6144]{1,0:T(8,128)(2,1)} %halo_attention.1) | data formatting | bytes 3145728

commit v3 on v2

--- a/solution.py
+++ b/solution.py
@@ -19,7 +19,10 @@
 RUN = 3
 LAGS_IN = (0, 2, 1, 3)
 LAGS_TOP = (1, 3, 5, 6)
+AHEAD = 3
 LAGS_HELD = (3, 1, 0)
+LAG_LATE = 8
+TURNS = 4
 MESH = pl.DeviceIdType.MESH
 
 
@@ -41,12 +44,14 @@
     onward = ctx < n_ctx - 1
     edge_far = edge & onward & (lane == 0)
     edge_near = edge & onward & (lane == 1)
-    keeper = top & (col == RUN - 1) & onward & (lane == 0)
-    holder = chip - (n_chip - RUN)
-    after = chip + (n_chip - RUN + 1)
-
-    def core(target):
-        return (target // n_chip, lax.rem(target, n_chip) * 2 + lane)
+    keeper = (row == 1) & (col == RUN - 1) & onward & (lane == 0)
+    to_keeper = n_chip - 2 * RUN
+    from_keeper = n_chip - 2 * RUN + 1
+
+    def core(away):
+        there = place + away
+        wrap = (there >= n_chip).astype(jnp.int32) - (there < 0).astype(jnp.int32)
+        return (ctx + wrap, uly + 2 * away - 2 * n_chip * wrap)
 
     pair_id = (ctx, uly + 1 - 2 * lane)
 
@@ -91,13 +96,33 @@
             device_id_type=MESH,
         )
 
+    def push_spare(h):
+        return pltpu.make_async_remote_copy(
+            src_ref=kv.at[h, :, rows(6), :],
+            dst_ref=held.at[h, 0],
+            send_sem=push_send.at[2, h],
+            recv_sem=held_recv.at[0, h],
+            device_id=core(-to_spare),
+            device_id_type=MESH,
+        )
+
+    def release_spare(h):
+        return pltpu.make_async_remote_copy(
+            src_ref=held.at[h, 0],
+            dst_ref=kv.at[h, :, rows(0), :],
+            send_sem=held_send.at[0, h],
+            recv_sem=recv_sem.at[0, h],
+            device_id=core(from_spare),
+            device_id_type=MESH,
+        )
+
     def push_held(h, src, index):
         return pltpu.make_async_remote_copy(
             src_ref=kv.at[h, :, rows(src), :],
             dst_ref=held.at[h, src // 2 - 1],
             send_sem=push_send.at[index, h],
             recv_sem=held_recv.at[src // 2 - 1, h],
-            device_id=core(holder),
+            device_id=core(-to_keeper),
             device_id_type=MESH,
         )
 
@@ -108,7 +133,7 @@
             dst_ref=kv.at[h, :, rows(dst), :],
             send_sem=held_send.at[index, h],
             recv_sem=recv_sem.at[dst, h],
-            device_id=core(after),
+            device_id=core(from_keeper),
             device_id_type=MESH,
         )
 
@@ -125,10 +150,21 @@
 
     own_next = jnp.logical_not(edge) | edge_near
     own_row = row < last_row
+    plane_out = lax.rem(ctx, TURNS) == TURNS - 1
+    plane_in = lax.rem(ctx, TURNS) == 0
+    direct = edge_near & jnp.logical_not(plane_out)
+    chained = top & (col == 0) & (lane == 0)
+    chained_two = top & (col == 0) & ((lane == 0) | plane_in)
+    cross_plane = plane_out & onward
+    spare_source = (row == last_row) & (col == 0) & cross_plane
+    spare_keeper = (row == 1 + lane) & (col == 0) & cross_plane
+    to_spare = (last_row - 1 - lane) * RUN
+    from_spare = n_chip - (1 + lane) * RUN
     own_skip = (col == RUN - 1) & (own_row | edge_near)
-    relay_up = (col == 1) | (top & (col == 0) & (lane == 0)) | edge_near
-    relay_two = edge_near
-    relay_three = (top & (col == 1)) | (top & (col == 0) & (lane == 0)) | edge_near
+    relay_up = (col == 1) | chained | edge_near
+    relay_two = direct
+    relay_three = (top & (col == 1)) | chained_two | direct
+    far_three = edge_far & jnp.logical_not(plane_out)
     relay_down = inner & (col == 1)
 
     barrier = pltpu.get_barrier_semaphore()
@@ -140,12 +176,14 @@
 
     head_of_block = top & (col == 0)
     has_back = ctx > 0
-    greet((chip >= 1) & jnp.logical_not(head_of_block & (lane == 0)), chip - 1)
-    greet(inner, chip - RUN)
-    greet((inner & (col == 1)) | (top & (col == 1) & has_back & (lane == 1)), chip - 2)
-    greet(inner & (col == 0), chip + 1)
-    greet(keeper, chip + (n_chip - RUN))
-    greet(head_of_block & has_back & (lane == 0), chip - (n_chip - RUN + 1))
+    greet((chip >= 1) & jnp.logical_not(head_of_block & (lane == 0)), -1)
+    greet(inner, -RUN)
+    greet((inner & (col == 1)) | (top & (col == 1) & has_back & (lane == 1)), -2)
+    greet(inner & (col == 0), 1)
+    greet(keeper, to_keeper)
+    greet(spare_keeper, to_spare)
+    greet(head_of_block & has_back & plane_in, -from_spare)
+    greet(head_of_block & has_back & (lane == 0), -from_keeper)
     pl.semaphore_signal(barrier, inc=1, device_id=pair_id, device_id_type=MESH)
     expected = (
         1
@@ -155,6 +193,8 @@
         + relay_down.astype(jnp.int32)
         + edge_far.astype(jnp.int32)
         + keeper.astype(jnp.int32)
+        + spare_source.astype(jnp.int32)
+        + spare_keeper.astype(jnp.int32)
     )
     pl.semaphore_wait(barrier, expected)
 
@@ -164,7 +204,11 @@
 
         @pl.when(own_next)
         def _():
-            push(h, 6, 4, 0, chip + 1).start()
+            push(h, 6, 4, 0, 1).start()
+
+        @pl.when(spare_source)
+        def _():
+            push_spare(h).start()
 
         @pl.when(edge_far)
         def _():
@@ -172,20 +216,22 @@
 
         @pl.when(own_skip)
         def _():
-            push(h, 6, 2, 2, chip + 2).start()
+            push(h, 6, 2, 2, 2).start()
 
         @pl.when(own_row)
         def _():
-            push(h, 6, 0, 1, chip + 3).start()
+            push(h, 6, 0, 1, 3).start()
 
         @pl.when(lane == 0)
         def _():
             across(h, 0).start()
 
     def received(h, slot):
-        push(h, 6, slot, 0, chip).wait_recv()
-
-    upfront = jnp.where((col == 1) & inner, 2, KV)
+        push(h, 6, slot, 0, 0).wait_recv()
+
+    late_edge = edge & cross_plane
+    early_own = (row == last_row) & (col == 1) & cross_plane
+    upfront = jnp.where(((col == 1) & inner & jnp.logical_not(early_own)) | edge, AHEAD, KV)
 
     def first_sends(h, carry):
         send_own(h)
@@ -218,26 +264,28 @@
         q_all = jnp.concatenate(
             [qbuf[:, pl.ds(pl.multiple_of(base + r * HEAD, HEAD), HEAD)] for r in range(PER)], axis=0
         )
-        for first in range(0, WINDOW, 256):
-            width = min(256, WINDOW - first)
-            block = lax.dot_general(
-                q_all, kv[h, 0, first : first + width, :], (((1,), (1,)), ((), ())),
-                preferred_element_type=jnp.float32,
-            )
-            for r in range(PER):
-                s_ref[r * CHUNK : (r + 1) * CHUNK, first : first + width] = (
-                    block[r * CHUNK : (r + 1) * CHUNK] + bias[:, first : first + width]
+        for part in range(0, PER * CHUNK, 384):
+            for first in range(0, WINDOW, 256):
+                width = min(256, WINDOW - first)
+                block = lax.dot_general(
+                    q_all[part : part + 384], kv[h, 0, first : first + width, :], (((1,), (1,)), ((), ())),
+                    preferred_element_type=jnp.float32,
                 )
-        totals = []
-        step = 32
-        for r in range(0, PER * CHUNK, step):
-            scores = s_ref[r : r + step, :]
-            peak = jnp.max(scores, axis=-1, keepdims=True)
-            weights = jnp.exp2((scores - peak) * SCALE2)
-            totals.append(jnp.sum(weights, axis=-1, keepdims=True))
-            p_ref[r : r + step, :] = weights.astype(jnp.bfloat16)
-        mixed = jnp.dot(p_ref[...], kv[h, 1], preferred_element_type=jnp.float32)
-        done = (mixed / jnp.concatenate(totals, axis=0)).astype(jnp.bfloat16)
+                for r in range(0, 384, CHUNK):
+                    s_ref[part + r : part + r + CHUNK, first : first + width] = (
+                        block[r : r + CHUNK] * SCALE2 + bias[:, first : first + width]
+                    )
+        done = []
+        for top_row in range(0, PER * CHUNK, 384):
+            totals = []
+            for r in range(top_row, top_row + 384, 32):
+                scores = s_ref[r : r + 32, :]
+                weights = jnp.exp2(scores - jnp.max(scores, axis=-1, keepdims=True))
+                totals.append(jnp.sum(weights, axis=-1, keepdims=True))
+                p_ref[r : r + 32, :] = weights.astype(jnp.bfloat16)
+            mixed = jnp.dot(p_ref[top_row : top_row + 384, :], kv[h, 1], preferred_element_type=jnp.float32)
+            done.append((mixed / jnp.concatenate(totals, axis=0)).astype(jnp.bfloat16))
+        done = jnp.concatenate(done, axis=0)
         for r in range(PER):
             obuf[:, pl.ds(pl.multiple_of(base + r * HEAD, HEAD), HEAD)] = done[r * CHUNK : (r + 1) * CHUNK]
         out_copy(h).start()
@@ -249,7 +297,7 @@
 
             @pl.when(relay_up)
             def _():
-                push(h, 4, 2, 3, chip + 1).start()
+                push(h, 4, 2, 3, 1).start()
 
             @pl.when(edge_far)
             def _():
@@ -257,7 +305,7 @@
 
             @pl.when(relay_two)
             def _():
-                push(h, 4, 0, 4, chip + 2).start()
+                push(h, 4, 0, 4, 2).start()
 
             across(h, 1 - lane).start()
 
@@ -268,9 +316,9 @@
 
             @pl.when(relay_three)
             def _():
-                push(h, 2, 0, 5, chip + 1).start()
-
-            @pl.when(edge_far)
+                push(h, 2, 0, 5, 1).start()
+
+            @pl.when(far_three)
             def _():
                 push_held(h, 2, 5).start()
 
@@ -283,7 +331,7 @@
 
             @pl.when(relay_down)
             def _():
-                push(h, 0, 2, 6, chip - 1).start()
+                push(h, 0, 2, 6, -1).start()
 
             @pl.when(lane == 1)
             def _():
@@ -293,6 +341,10 @@
         push_held(h, 2 * index + 2, 0).wait_recv()
         release(h, index).start()
 
+    def on_spare(h):
+        push_spare(h).wait_recv()
+        release_spare(h).start()
+
     def inside(h):
         return (h >= 0) & (h < KV)
 
@@ -305,9 +357,9 @@
             action(h)
 
     lag_near = jnp.where(top, LAGS_TOP[0], LAGS_IN[0])
-    lag_middle = jnp.where(top, LAGS_TOP[1], LAGS_IN[1])
-    lag_far = jnp.where(top, LAGS_TOP[2], LAGS_IN[2])
-    lag_attend = jnp.where(top, LAGS_TOP[3], LAGS_IN[3])
+    lag_middle = jnp.where(top, LAGS_TOP[1], jnp.where(late_edge, LAG_LATE, LAGS_IN[1]))
+    lag_far = jnp.where(top, LAGS_TOP[2], jnp.where(late_edge, LAG_LATE, LAGS_IN[2]))
+    lag_attend = jnp.where(top, LAGS_TOP[3], jnp.where(late_edge, LAG_LATE + 1, LAGS_IN[3]))
 
     def finish(h):
         for stage in range(3):
@@ -319,30 +371,37 @@
     def step(t, carry):
         at(t, -upfront, send_own)
         at(t, lag_near, on_near)
-        at(t, LAGS_HELD[2], lambda h: on_held(h, 2), keeper)
-        at(t, LAGS_HELD[1], lambda h: on_held(h, 1), keeper)
-        at(t, LAGS_HELD[0], lambda h: on_held(h, 0), keeper)
+        at(2 * t, 0, on_spare, spare_keeper)
+        at(2 * t, -1, on_spare, spare_keeper)
+        at(t, LAGS_HELD[2], lambda h: on_held(h, 2), keeper & jnp.logical_not(plane_out))
+        at(t, LAGS_HELD[1], lambda h: on_held(h, 1), keeper & jnp.logical_not(plane_out))
+        for more in range(2):
+            at(2 * t, -more, lambda h: on_held(h, 2), keeper & plane_out)
+            at(2 * t, 1 - more, lambda h: on_held(h, 1), keeper & plane_out)
+        at(t, LAGS_HELD[0], lambda h: on_held(h, 0), keeper & jnp.logical_not(plane_out))
         at(t, lag_far, on_far, inner)
         at(t, lag_middle, on_middle)
         at(t, lag_far, on_far, top)
         at(t, lag_attend, finish)
         return carry
 
-    lax.fori_loop(0, KV + lag_attend, step, 0)
+    lax.fori_loop(0, KV + jnp.maximum(lag_attend, LAGS_HELD[0]), step, 0)
 
     def drain(h, carry):
         sends = (
-            (0, own_next | edge_far), (1, own_row), (2, own_skip),
+            (0, own_next | edge_far), (1, own_row), (2, own_skip | spare_source),
             (3, (chip >= 1) & (relay_up | edge_far)), (4, relay_two),
-            (5, (chip >= 2) & (relay_three | edge_far)), (6, relay_down),
+            (5, (chip >= 2) & (relay_three | far_three)), (6, relay_down),
         )
         for index, cond in sends:
             @pl.when(cond)
             def _():
-                push(h, 6, 4, index, chip).wait_send()
+                push(h, 6, 4, index, 0).wait_send()
 
         for index in range(3):
-            @pl.when(keeper)
+            held_here = keeper if index else (keeper & jnp.logical_not(plane_out)) | spare_keeper
+
+            @pl.when(held_here)
             def _():
                 release(h, index).wait_send()
 

time: 60.7 us -> 56.4 us (0.929)
  the two profiles are of different devices: /device:TPU:40 before, /device:TPU:104 now
where the time goes in v3:
time: 56.4 us; the launch traced here: 56.2 us
  Pallas kernels  53.5 us (95%)
  local copies, waits for them, and re-layouts  2.69 us (5%)
    pallas_call x1, Pallas kernels, shards(): pl.pallas_call(lambda *refs: kernel(n_ctx, n_chip, *refs), out_shape=jax....  53.5 us
    unnamed x1, local copies, waits for them, and re-layouts  2.69 us

profile of v3, /device:TPU:104, one launch (start us, length us, event | category | flops | bytes accessed | tf_op | source)
XLA Modules:
  0.0 56.2 jit_solution(18129745986950422776)
XLA Ops:
  0.0 53.5 %halo_attention.1 = bf16[128,6144]{1,0:T(8,128)(2,1)} custom-call(bf16[128,6144]{1,0:T(8,128)(2,1)} %refs_0_.1, bf16[128,1024]{1,0:T(8,128)(2,1)} %refs_1_.1, bf16[128,1024]{1,0:T(8,128)(2,1)} %refs_2_.1, s32[768,128]{1,0:T(8,128)} %bitcast.1), custom_call_target="tpu_custom_call" | custom-call | tf_op jit(solution)/shard_map/halo_attention/pallas_call | solution.py:423
  53.5 2.7 %copy.6 = bf16[128,6144]{1,0:T(8,128)(2,1)} copy(bf16[128,6144]{1,0:T(8,128)(2,1)} %halo_attention.1) | data formatting | bytes 3145728

commit v4 on v3

--- a/solution.py
+++ b/solution.py
@@ -231,7 +231,7 @@
 
     late_edge = edge & cross_plane
     early_own = (row == last_row) & (col == 1) & cross_plane
-    upfront = jnp.where(((col == 1) & inner & jnp.logical_not(early_own)) | edge, AHEAD, KV)
+    upfront = jnp.where(((col == 1) & inner & jnp.logical_not(early_own)) | edge | spare_keeper, AHEAD, KV)
 
     def first_sends(h, carry):
         send_own(h)

time: 56.4 us -> 54.8 us (0.972)
  Pallas kernels: 53.5 us -> 51.9 us
    pallas_call x1, Pallas kernels: 53.5 us -> 51.9 us  [shards(): pl.pallas_call(lambda *refs: kernel(n_ctx, n_chip, *refs), out_shape=jax....]
where the time goes in v4:
time: 54.8 us; the launch traced here: 54.6 us
  Pallas kernels  51.9 us (95%)
  local copies, waits for them, and re-layouts  2.69 us (5%)
    pallas_call x1, Pallas kernels, shards(): pl.pallas_call(lambda *refs: kernel(n_ctx, n_chip, *refs), out_shape=jax....  51.9 us
    unnamed x1, local copies, waits for them, and re-layouts  2.69 us

profile of v4, /device:TPU:104, one launch (start us, length us, event | category | flops | bytes accessed | tf_op | source)
XLA Modules:
  0.0 54.6 jit_solution(1971610230399414704)
XLA Ops:
  0.0 51.9 %halo_attention.1 = bf16[128,6144]{1,0:T(8,128)(2,1)} custom-call(bf16[128,6144]{1,0:T(8,128)(2,1)} %refs_0_.1, bf16[128,1024]{1,0:T(8,128)(2,1)} %refs_1_.1, bf16[128,1024]{1,0:T(8,128)(2,1)} %refs_2_.1, s32[768,128]{1,0:T(8,128)} %bitcast.1), custom_call_target="tpu_custom_call" | custom-call | tf_op jit(solution)/shard_map/halo_attention/pallas_call | solution.py:423
  51.9 2.7 %copy.6 = bf16[128,6144]{1,0:T(8,128)(2,1)} copy(bf16[128,6144]{1,0:T(8,128)(2,1)} %halo_attention.1) | data formatting | bytes 3145728
